TPU v7x, 32 devices: a whole 2x2x4 slice. The times are simulated.
32 devices in a mesh: layer: 8 (over z, x), land: 4 (over y, core).
Axes of the slice: x: 2, y: 2, z: 4, core: 2. Of those that a mesh axis runs over, the one named last changes fastest.
Arguments:
- gradients: bfloat16 [960, 65536], P(None, ('layer', 'land')), may hold values from -6 to 6
- queries: bfloat16 [32, 65536], P(None, ('layer', 'land')), may hold values from -6 to 6
- landmarks: bfloat16 [1024, 65536], P(None, ('layer', 'land')), may hold values from -0.0234375 to 0.0234375
- whitening: bfloat16 [1024, 1024], P(None, 'land'), may hold values from -2.5 to 2.5
Outputs:
- scores: float32 [32, 960], P('land', 'layer')
All inputs are finite; a program needn't handle non-finite values.
Results may differ from a plain program's by a relative error of at most 0.023.
Values may be sent and summed in bfloat16 or wider, within the bound.
A program may use at most 128 MiB of HBM per device.

v0:
```python
import jax
import jax.numpy as jnp
from jax import lax
from jax.sharding import PartitionSpec as P

NN = (((1,), (0,)), ((), ()))
NT = (((1,), (1,)), ((), ()))


def dot(a, b, dims):
    return lax.dot_general(a, b, dims, preferred_element_type=jnp.float32)


def local(gradients, queries, landmarks, whitening):
    half = jnp.bfloat16
    factor = landmarks.shape[0] ** (-0.5)
    partial = dot(queries, landmarks, NT).astype(half)
    query_proj = lax.psum(partial, ("layer", "land"))
    query_white = dot(query_proj, whitening, NN).astype(half)
    back = lax.psum(dot(query_white, whitening, NT).astype(half), "land")
    spread = dot(back, landmarks, NN).astype(half)
    scores = dot(spread, gradients, NT) * factor
    share = lax.psum_scatter(scores.astype(half), "layer", scatter_dimension=1, tiled=True)
    return lax.psum_scatter(share, "land", scatter_dimension=0, tiled=True).astype(jnp.float32)


def solution(mesh):
    return jax.shard_map(
        local,
        mesh=mesh,
        in_specs=(
            P(None, ("layer", "land")),
            P(None, ("layer", "land")),
            P(None, ("layer", "land")),
            P(None, "land"),
        ),
        out_specs=P("land", "layer"),
        check_vma=False,
    )
```

profile of v0, /device:TPU:0, one launch (start us, length us, event | category | flops | bytes accessed | tf_op | source)
XLA Modules:
  0.0 224.0 jit_solution(2773502246041843266)
XLA Ops:
  6.5 0.0 copy-start
  6.5 0.0 copy-start.2
  6.5 0.0 copy-start.1
  6.5 0.0 all-reduce.5.cloned.1.call-start
  6.5 4.3 %convolution_convert_fusion.2 = bf16[32,1024]{1,0:T(8,128)(2,1)} fusion(bf16[32,2048]{1,0:T(8,128)(2,1)} %param.5, bf16[1024,2048]{1,0:T(8,128)(2,1)} %param.6), kind=kOutput, calls=%fused_computation.5 | convolution fusion | flops 134250496 | bytes 4390912 | tf_op jit(solution)/shard_map/dot_general | solution.py:11
  10.8 0.0 all-reduce.5.cloned.1.call-update
  10.9 0.0 all-reduce.7.cloned.1.call-start
  10.9 122.3 %all-reduce.5.cloned.1.call-done = bf16[32,1024]{1,0:T(8,128)(2,1)} async-done(((bf16[32,1024]{1,0:T(8,128)(2,1)}), bf16[32,1024]{1,0:T(8,128)(2,1)}) %all-reduce.5.cloned.1.call-update) | async-done | bytes 65552 | tf_op jit(solution)/shard_map/psum | solution.py:18
  133.2 0.0 copy-done
  133.2 2.0 convolution_convert_fusion.1
  135.2 0.0 all-reduce.7.cloned.1.call-update
  135.2 0.0 copy-done.2
  135.2 0.6 dynamic-slice
  135.8 0.0 copy-done.1
  135.8 0.6 dynamic-slice.2
  137.6 29.8 %all-reduce.7.cloned.1.call-done = bf16[32,1024]{1,0:T(8,128)(2,1)} async-done(((bf16[32,1024]{1,0:T(8,128)(2,1)}), bf16[32,1024]{1,0:T(8,128)(2,1)}) %all-reduce.7.cloned.1.call-update) | async-done | bytes 65552 | tf_op jit(solution)/shard_map/psum | solution.py:20
  167.4 5.4 %fusion.2 = bf16[32,960]{1,0:T(8,128)(2,1)S(1)} fusion(bf16[960,2048]{1,0:T(8,128)(2,1)} %param.4, bf16[32,1024]{1,0:T(8,128)(2,1)} %all-reduce.7.cloned.1.call-done, bf16[1024,2048]{1,0:T(8,128)(2,1)} %param.6), kind=kOutput, calls=%fused_computation.3 | convolution fusion | flops 260173824 | bytes 8253440 | tf_op jit(solution)/shard_map/dot_general | solution.py:11
  172.8 37.5 %all-reduce = bf16[32,960]{1,0:T(8,128)(2,1)S(1)} all-reduce(bf16[32,960]{1,0:T(8,128)(2,1)S(1)} %fusion.2), channel_id=2, replica_groups=mesh['layer'=8,'land'=4] {'layer'}, use_global_device_ids=true, to_apply=%region_2.0.clone | all-reduce | flops 30720 | bytes 122880
  210.3 0.1 constant_dynamic-slice_fusion
  210.4 6.1 %all-reduce.1 = bf16[32,120]{1,0:T(8,128)(2,1)S(1)} all-reduce(bf16[32,120]{1,0:T(8,128)(2,1)S(1)} %constant_dynamic-slice_fusion), channel_id=3, replica_groups=mesh['layer'=8,'land'=4] {'land'}, use_global_device_ids=true, to_apply=%region_3.0.clone | all-reduce | flops 3840 | bytes 15360
  216.5 0.6 dynamic-slice_convert_fusion
Async XLA Ops:
  6.5 126.7 %copy-start = (bf16[1024,256]{1,0:T(8,128)(2,1)S(1)}, bf16[1024,256]{1,0:T(8,128)(2,1)}, u32[]{:S(2)}) copy-start(bf16[1024,256]{1,0:T(8,128)(2,1)} %param.7) | copy-start | bytes 1572868
  6.5 128.7 %copy-start.2 = (u32[32]{0:T(128)S(1)}, u32[32]{0:T(128)}, u32[]{:S(2)}) copy-start(u32[32]{0:T(128)} %constant.4) | copy-start | bytes 388
  6.5 129.3 %copy-start.1 = (u32[32]{0:T(128)S(1)}, u32[32]{0:T(128)}, u32[]{:S(2)}) copy-start(u32[32]{0:T(128)} %constant.8) | copy-start | bytes 388
  6.5 126.7 %all-reduce.5.cloned.1.call-start = ((), (), s32[]{:S(2)}) async-start(), calls=%async_computation | async-start | bytes 131072 | tf_op jit(solution)/shard_map/psum | solution.py:18
  10.9 156.6 %all-reduce.7.cloned.1.call-start = ((), (), s32[]{:S(2)}) async-start(), calls=%async_computation.1 | async-start | bytes 131072 | tf_op jit(solution)/shard_map/psum | solution.py:20
Sparse Core Ops, SparseCore 0:
  12.9 120.2 all-reduce.4
  135.5 31.8 all-reduce.6
where the time goes:
time: 224 us
  waiting for transfers between devices  152 us (68%)
  blocking collectives  43.6 us (19%)
  between operations  14.7 us (7%)
  matrix products  11.6 us (5%)
    psum x1, waiting for transfers between devices, local(): query_proj = lax.psum(partial, ('layer', 'land'))  122 us
    unnamed x2, blocking collectives  43.6 us
    psum x1, waiting for transfers between devices, local(): back = lax.psum(dot(query_white, whitening, NT).astype(half), 'land')  29.8 us
    dot_general x3, matrix products, dot(): return lax.dot_general(a, b, dims, preferred_element_type=jnp.float32)  11.6 us
  transfers between devices with their start and end apart: 2, of which 2 were waited for; matrix products, arithmetic and copies ran while one was open for 1% of the time, Pallas kernels for 0%

commit v1 on v0

--- a/solution.py
+++ b/solution.py
@@ -17,7 +17,8 @@
     partial = dot(queries, landmarks, NT).astype(half)
     query_proj = lax.psum(partial, ("layer", "land"))
     query_white = dot(query_proj, whitening, NN).astype(half)
-    back = lax.psum(dot(query_white, whitening, NT).astype(half), "land")
+    u_in = dot(query_white, whitening, NT).astype(half)
+    back = jnp.sum(jax.lax.all_gather(u_in, axis_name="land"), axis=0)
     spread = dot(back, landmarks, NN).astype(half)
     scores = dot(spread, gradients, NT) * factor
     share = lax.psum_scatter(scores.astype(half), "layer", scatter_dimension=1, tiled=True)

time: 224 us -> 197 us (0.88)
  waiting for transfers between devices: 152 us -> 120 us
  blocking collectives: 43.6 us -> 49.6 us
    psum x1 -> x0, waiting for transfers between devices: 29.8 us -> none  [local(): back = lax.psum(dot(query_white, whitening, NT).astype(half), 'land')]
    all_gather x0 -> x1, blocking collectives: none -> 7.13 us  [local(): back = jnp.sum(jax.lax.all_gather(u_in, axis_name='land'), axis=0)]
    psum x1, waiting for transfers between devices: 122 us -> 120 us  [local(): query_proj = lax.psum(partial, ('layer', 'land'))]
  transfers between devices with their start and end apart: 2 -> 1, of which waited for: 2 -> 1; matrix products, arithmetic and copies ran while one was open for 1% -> 1% of each run, Pallas kernels for 0% -> 0%
where the time goes in v1:
time: 197 us
  waiting for transfers between devices  120 us (61%)
  blocking collectives  49.6 us (25%)
  between operations  14.6 us (7%)
  matrix products  10.9 us (6%)
    psum x1, waiting for transfers between devices, local(): query_proj = lax.psum(partial, ('layer', 'land'))  120 us
    unnamed x2, blocking collectives  42.5 us
    dot_general x3, matrix products, dot(): return lax.dot_general(a, b, dims, preferred_element_type=jnp.float32)  10.9 us
    all_gather x1, blocking collectives, local(): back = jnp.sum(jax.lax.all_gather(u_in, axis_name='land'), axis=0)  7.13 us
  transfers between devices with their start and end apart: 1, of which 1 were waited for; matrix products, arithmetic and copies ran while one was open for 1% of the time, Pallas kernels for 0%

profile of v1, /device:TPU:0, one launch (start us, length us, event | category | flops | bytes accessed | tf_op | source)
XLA Modules:
  0.0 197.1 jit_solution(12049667483593894838)
XLA Ops:
  6.5 0.0 copy-start
  6.5 0.0 copy-start.2
  6.5 0.0 copy-start.1
  6.5 0.0 all-reduce.4.cloned.1.call-start
  6.5 4.3 %convolution_convert_fusion.2 = bf16[32,1024]{1,0:T(8,128)(2,1)} fusion(bf16[32,2048]{1,0:T(8,128)(2,1)} %param.5, bf16[1024,2048]{1,0:T(8,128)(2,1)} %param.6), kind=kOutput, calls=%fused_computation.5 | convolution fusion | flops 134250496 | bytes 4390912 | tf_op jit(solution)/shard_map/dot_general | solution.py:11
  10.8 0.0 all-reduce.4.cloned.1.call-update
  10.9 0.0 copy-done.2
  10.9 0.6 dynamic-slice
  11.4 0.0 copy-done.1
  11.5 0.6 dynamic-slice.2
  13.2 120.0 %all-reduce.4.cloned.1.call-done = bf16[32,1024]{1,0:T(8,128)(2,1)} async-done(((bf16[32,1024]{1,0:T(8,128)(2,1)}), bf16[32,1024]{1,0:T(8,128)(2,1)}) %all-reduce.4.cloned.1.call-update) | async-done | bytes 65552 | tf_op jit(solution)/shard_map/psum | solution.py:18
  133.2 0.0 copy-done
  133.2 1.3 convolution_convert_fusion.1
  134.5 7.1 %all-gather = bf16[128,1024]{1,0:T(8,128)(2,1)S(1)} all-gather(bf16[32,1024]{1,0:T(8,128)(2,1)S(1)} %convolution_convert_fusion.1), channel_id=2, replica_groups=mesh['layer'=8,'land'=4] {'land'}, dimensions={0}, use_global_device_ids=true | all-gather | bytes 327680 | tf_op jit(solution)/shard_map/all_gather | solution.py:21
  141.7 5.3 %fusion.2 = bf16[32,960]{1,0:T(8,128)(2,1)S(1)} fusion(bf16[960,2048]{1,0:T(8,128)(2,1)} %param.4, bf16[32,1024]{1,0:T(8,128)(2,1)S(1)} %reduce_sum.12, bf16[1024,2048]{1,0:T(8,128)(2,1)} %param.6), kind=kOutput, calls=%fused_computation.3 | convolution fusion | flops 260173824 | bytes 8253440 | tf_op jit(solution)/shard_map/dot_general | solution.py:11
  147.1 36.4 %all-reduce = bf16[32,960]{1,0:T(8,128)(2,1)S(1)} all-reduce(bf16[32,960]{1,0:T(8,128)(2,1)S(1)} %fusion.2), channel_id=3, replica_groups=mesh['layer'=8,'land'=4] {'layer'}, use_global_device_ids=true, to_apply=%region_2.0.clone | all-reduce | flops 30720 | bytes 122880
  183.5 0.1 constant_dynamic-slice_fusion
  183.6 6.1 %all-reduce.1 = bf16[32,120]{1,0:T(8,128)(2,1)S(1)} all-reduce(bf16[32,120]{1,0:T(8,128)(2,1)S(1)} %constant_dynamic-slice_fusion), channel_id=4, replica_groups=mesh['layer'=8,'land'=4] {'land'}, use_global_device_ids=true, to_apply=%region_3.0.clone | all-reduce | flops 3840 | bytes 15360
  189.6 0.6 dynamic-slice_convert_fusion
  (1 shorter events, 0.0 us)
Async XLA Ops:
  6.5 126.7 %copy-start = (bf16[1024,256]{1,0:T(8,128)(2,1)S(1)}, bf16[1024,256]{1,0:T(8,128)(2,1)}, u32[]{:S(2)}) copy-start(bf16[1024,256]{1,0:T(8,128)(2,1)} %param.7) | copy-start | bytes 1572868
  6.5 4.3 %copy-start.2 = (u32[32]{0:T(128)S(1)}, u32[32]{0:T(128)}, u32[]{:S(2)}) copy-start(u32[32]{0:T(128)} %constant.7) | copy-start | bytes 388
  6.5 4.9 %copy-start.1 = (u32[32]{0:T(128)S(1)}, u32[32]{0:T(128)}, u32[]{:S(2)}) copy-start(u32[32]{0:T(128)} %constant.11) | copy-start | bytes 388
  6.5 126.7 %all-reduce.4.cloned.1.call-start = ((), (), s32[]{:S(2)}) async-start(), calls=%async_computation | async-start | bytes 131072 | tf_op jit(solution)/shard_map/psum | solution.py:18
Sparse Core Ops, SparseCore 0:
  12.9 120.2 all-reduce.3

commit v2 on v0

--- a/solution.py
+++ b/solution.py
@@ -2,6 +2,7 @@
 import jax.numpy as jnp
 from jax import lax
 from jax.sharding import PartitionSpec as P
+from jax.lax import psum
 
 NN = (((1,), (0,)), ((), ()))
 NT = (((1,), (1,)), ((), ()))
@@ -15,7 +16,7 @@
     half = jnp.bfloat16
     factor = landmarks.shape[0] ** (-0.5)
     partial = dot(queries, landmarks, NT).astype(half)
-    query_proj = lax.psum(partial, ("layer", "land"))
+    query_proj = psum(psum(partial, "land"), "layer")
     query_white = dot(query_proj, whitening, NN).astype(half)
     back = lax.psum(dot(query_white, whitening, NT).astype(half), "land")
     spread = dot(back, landmarks, NN).astype(half)

time: 224 us -> 207 us (0.924)
  waiting for transfers between devices: 152 us -> 135 us
    psum x1 -> x2, waiting for transfers between devices: 122 us -> 106 us  [local(): query_proj = psum(psum(partial, 'land'), 'layer')]
  transfers between devices with their start and end apart: 2 -> 3, of which waited for: 2 -> 3; matrix products, arithmetic and copies ran while one was open for 1% -> 1% of each run, Pallas kernels for 0% -> 0%
where the time goes in v2:
time: 207 us
  waiting for transfers between devices  135 us (65%)
  blocking collectives  43.6 us (21%)
  between operations  14.4 us (7%)
  matrix products  11.6 us (6%)
    psum x2, waiting for transfers between devices, local(): query_proj = psum(psum(partial, 'land'), 'layer')  106 us
    unnamed x2, blocking collectives  43.6 us
    psum x1, waiting for transfers between devices, local(): back = lax.psum(dot(query_white, whitening, NT).astype(half), 'land')  29.1 us
    dot_general x3, matrix products, dot(): return lax.dot_general(a, b, dims, preferred_element_type=jnp.float32)  11.6 us
  transfers between devices with their start and end apart: 3, of which 3 were waited for; matrix products, arithmetic and copies ran while one was open for 1% of the time, Pallas kernels for 0%

profile of v2, /device:TPU:0, one launch (start us, length us, event | category | flops | bytes accessed | tf_op | source)
XLA Modules:
  0.0 206.8 jit_solution(174283497223842191)
XLA Ops:
  6.5 0.0 copy-start
  6.5 0.0 copy-start.2
  6.5 0.0 copy-start.1
  6.5 0.0 all-reduce.6.cloned.1.call-start
  6.5 4.3 %convolution_convert_fusion.2 = bf16[32,1024]{1,0:T(8,128)(2,1)} fusion(bf16[32,2048]{1,0:T(8,128)(2,1)} %param.5, bf16[1024,2048]{1,0:T(8,128)(2,1)} %param.6), kind=kOutput, calls=%fused_computation.5 | convolution fusion | flops 134250496 | bytes 4390912 | tf_op jit(solution)/shard_map/dot_general | solution.py:12
  10.8 0.0 all-reduce.6.cloned.1.call-update
  10.8 0.0 all-reduce.8.cloned.1.call-start
  10.9 33.8 %all-reduce.6.cloned.1.call-done = bf16[32,1024]{1,0:T(8,128)(2,1)} async-done(((bf16[32,1024]{1,0:T(8,128)(2,1)}), bf16[32,1024]{1,0:T(8,128)(2,1)}) %all-reduce.6.cloned.1.call-update) | async-done | bytes 65552 | tf_op jit(solution)/shard_map/psum | solution.py:19
  44.7 0.0 all-reduce.8.cloned.1.call-update
  44.8 0.0 all-reduce.10.cloned.1.call-start
  44.8 72.2 %all-reduce.8.cloned.1.call-done = bf16[32,1024]{1,0:T(8,128)(2,1)} async-done(((bf16[32,1024]{1,0:T(8,128)(2,1)}), bf16[32,1024]{1,0:T(8,128)(2,1)}) %all-reduce.8.cloned.1.call-update) | async-done | bytes 65552 | tf_op jit(solution)/shard_map/psum | solution.py:19
  117.1 0.0 copy-done
  117.1 2.0 convolution_convert_fusion.1
  119.0 0.0 all-reduce.10.cloned.1.call-update
  119.1 0.0 copy-done.2
  119.1 0.6 dynamic-slice
  119.7 0.0 copy-done.1
  119.7 0.6 dynamic-slice.2
  121.5 29.1 %all-reduce.10.cloned.1.call-done = bf16[32,1024]{1,0:T(8,128)(2,1)} async-done(((bf16[32,1024]{1,0:T(8,128)(2,1)}), bf16[32,1024]{1,0:T(8,128)(2,1)}) %all-reduce.10.cloned.1.call-update) | async-done | bytes 65552 | tf_op jit(solution)/shard_map/psum | solution.py:21
  150.5 5.4 %fusion.2 = bf16[32,960]{1,0:T(8,128)(2,1)S(1)} fusion(bf16[960,2048]{1,0:T(8,128)(2,1)} %param.4, bf16[32,1024]{1,0:T(8,128)(2,1)} %all-reduce.10.cloned.1.call-done, bf16[1024,2048]{1,0:T(8,128)(2,1)} %param.6), kind=kOutput, calls=%fused_computation.3 | convolution fusion | flops 260173824 | bytes 8253440 | tf_op jit(solution)/shard_map/dot_general | solution.py:12
  155.9 37.5 %all-reduce = bf16[32,960]{1,0:T(8,128)(2,1)S(1)} all-reduce(bf16[32,960]{1,0:T(8,128)(2,1)S(1)} %fusion.2), channel_id=2, replica_groups=mesh['layer'=8,'land'=4] {'layer'}, use_global_device_ids=true, to_apply=%region_3.0.clone | all-reduce | flops 30720 | bytes 122880
  193.4 0.1 constant_dynamic-slice_fusion
  193.5 6.1 %all-reduce.1 = bf16[32,120]{1,0:T(8,128)(2,1)S(1)} all-reduce(bf16[32,120]{1,0:T(8,128)(2,1)S(1)} %constant_dynamic-slice_fusion), channel_id=3, replica_groups=mesh['layer'=8,'land'=4] {'land'}, use_global_device_ids=true, to_apply=%region_4.0.clone | all-reduce | flops 3840 | bytes 15360
  199.6 0.6 dynamic-slice_convert_fusion
Async XLA Ops:
  6.5 110.5 %copy-start = (bf16[1024,256]{1,0:T(8,128)(2,1)S(1)}, bf16[1024,256]{1,0:T(8,128)(2,1)}, u32[]{:S(2)}) copy-start(bf16[1024,256]{1,0:T(8,128)(2,1)} %param.7) | copy-start | bytes 1572868
  6.5 112.5 %copy-start.2 = (u32[32]{0:T(128)S(1)}, u32[32]{0:T(128)}, u32[]{:S(2)}) copy-start(u32[32]{0:T(128)} %constant.4) | copy-start | bytes 388
  6.5 113.1 %copy-start.1 = (u32[32]{0:T(128)S(1)}, u32[32]{0:T(128)}, u32[]{:S(2)}) copy-start(u32[32]{0:T(128)} %constant.8) | copy-start | bytes 388
  6.5 38.2 %all-reduce.6.cloned.1.call-start = ((), (), s32[]{:S(2)}) async-start(), calls=%async_computation | async-start | bytes 131072 | tf_op jit(solution)/shard_map/psum | solution.py:19
  10.8 106.2 %all-reduce.8.cloned.1.call-start = ((), (), s32[]{:S(2)}) async-start(), calls=%async_computation.1 | async-start | bytes 131072 | tf_op jit(solution)/shard_map/psum | solution.py:19
  44.8 105.8 %all-reduce.10.cloned.1.call-start = ((), (), s32[]{:S(2)}) async-start(), calls=%async_computation.2 | async-start | bytes 131072 | tf_op jit(solution)/shard_map/psum | solution.py:21
Sparse Core Ops, SparseCore 0:
  11.0 33.7 all-reduce.5
  48.5 68.4 all-reduce.7
  119.5 30.9 all-reduce.9
